TPU v7x, 128 devices: a whole 4x4x4 slice. The times are simulated.
128 devices in a mesh: grp: 2 (over core), dev: 64 (over x, y, z).
Axes of the slice: x: 4, y: 4, z: 4, core: 2. Of those that a mesh axis runs over, the one named last changes fastest.
Arguments:
- residual_in: bfloat16 [2048, 2048], P(('grp', 'dev')), may hold values from -1.5 to 1.5
- queries: bfloat16 [2, 1024, 4096], P(None, 'dev', 'grp'), may hold values from -2.5 to 2.5
- latest_key_value: bfloat16 [2, 1024, 4, 256], P(None, 'dev', 'grp'), may hold values from -2.5 to 2.5
- key_value_cache: bfloat16 [2, 1024, 4, 256, 256], P(None, 'dev', 'grp'), may hold values from -2.5 to 2.5
- cache_len: int32 [2, 1024], P(None, 'dev'), may hold values from 1 to 256, 131072 in all within a row
- out_weight: bfloat16 [4096, 2048], P('grp'), may hold values from -0.09375 to 0.09375
- norm_gain: bfloat16 [2048], replicated, may hold values from 0.099609375 to 1.8984375
- router_weight: bfloat16 [2048, 128], replicated, may hold values from -0.125 to 0.125
- routes: int32 [2048, 8], P(('grp', 'dev')), may hold values from 0 to 127, all different within a row; in each aligned block of 16 rows (0 to 15, 16 to 31, ...) at most 2 rows name the same one
- expert_gate_up: bfloat16 [128, 2048, 1536], P(('grp', 'dev')), may hold values from -0.125 to 0.125
- expert_down: bfloat16 [128, 768, 2048], P(('grp', 'dev')), may hold values from -0.21875 to 0.21875
Outputs:
- layer_out: bfloat16 [2048, 2048], P(('grp', 'dev'))
Inputs may be any that keep to these rules, and one draw needn't show every extreme that they name: Each row of cache_len of 1024 entries sums to 131072, and its largest entry is exactly 256. `routes`: the 8 experts of a row are distinct; in each aligned block of 16 rows (the rows of one device) no expert is named by more than 2 rows, a bound that some block reaches.
All inputs are finite; a program needn't handle non-finite values. No bound on the sum of `cache_len` on one device may be relied on, other than what follows from the above.
Results may differ from a plain program's by a relative error of at most 0.017.
Values may be sent and summed in bfloat16 or wider, within the bound.
No kernel may reach another device: no remote copies, remote signals or barrier semaphores. Data moves between devices by JAX's collectives and lax.ppermute only.
A program may use at most 128 MiB of HBM per device.

v0:
```python
import math
import jax
import jax.numpy as jnp
from jax import lax
from jax.sharding import PartitionSpec as P

HEAD_SIZE = 128
FF = 768


def per_device(
    residual_in,
    queries,
    latest_key_value,
    key_value_cache,
    cache_len,
    out_weight,
    norm_gain,
    router_weight,
    routes,
    expert_gate_up,
    expert_down,
):
    halves = queries.shape[0]
    tokens = queries.shape[1]
    kv_heads = key_value_cache.shape[2]
    positions = key_value_cache.shape[3]
    q_heads = queries.shape[2] // HEAD_SIZE
    query_group = q_heads // kv_heads
    width = residual_in.shape[1]
    scale = 1.0 / math.sqrt(HEAD_SIZE)
    query_vector = queries.reshape(halves, tokens, kv_heads, query_group, HEAD_SIZE)
    scores = (
        jnp.einsum(
            "hrkgd,hrksd->hrkgs",
            query_vector,
            key_value_cache[..., :HEAD_SIZE],
            preferred_element_type=jnp.float32,
        )
        * scale
    )
    own_score = (
        jnp.einsum(
            "hrkgd,hrkd->hrkg",
            query_vector,
            latest_key_value[..., :HEAD_SIZE],
            preferred_element_type=jnp.float32,
        )
        * scale
    )
    visible = (
        jnp.arange(positions, dtype=jnp.int32)[None, None, None, None, :]
        < cache_len[:, :, None, None, None]
    )
    raised = jnp.where(visible, jnp.exp(scores), 0.0)
    own_raised = jnp.exp(own_score)
    totals = jnp.sum(raised, axis=-1) + own_raised
    weights = (raised / totals[..., None]).astype(jnp.bfloat16)
    own_weight = (own_raised / totals).astype(jnp.bfloat16)
    mixed = jnp.einsum(
        "hrkgs,hrksd->hrkgd",
        weights,
        key_value_cache[..., HEAD_SIZE:],
        preferred_element_type=jnp.float32,
    )
    mixed = (
        mixed
        + own_weight.astype(jnp.float32)[..., None]
        * latest_key_value[..., HEAD_SIZE:].astype(jnp.float32)[:, :, :, None, :]
    )
    attended = mixed.astype(jnp.bfloat16).reshape(halves * tokens, q_heads * HEAD_SIZE)
    partial_value = jnp.dot(attended, out_weight, preferred_element_type=jnp.float32).reshape(
        halves, tokens, width
    )
    summed = lax.psum(partial_value, "grp")
    projected = lax.dynamic_index_in_dim(summed, lax.axis_index("grp"), 0, keepdims=False)
    hidden = residual_in.astype(jnp.float32) + projected
    meansq = jnp.mean(hidden * hidden, axis=-1, keepdims=True)
    normed = (hidden * lax.rsqrt(meansq + 1e-06) * norm_gain.astype(jnp.float32)).astype(
        jnp.bfloat16
    )
    logits = jnp.dot(normed, router_weight, preferred_element_type=jnp.float32)
    picked = jnp.exp(jnp.take_along_axis(logits, routes, axis=1))
    gates = picked / jnp.sum(picked, axis=1, keepdims=True)
    batch_rows = routes.shape[0]
    topk = routes.shape[1]
    experts_all = router_weight.shape[1]
    capacity = max(2, 2 * batch_rows * topk // experts_all)
    flat_routes = routes.reshape(batch_rows * topk)
    onehot = (flat_routes[:, None] == jnp.arange(experts_all, dtype=jnp.int32)[None, :]).astype(
        jnp.int32
    )
    ranks = jnp.sum(onehot * (jnp.cumsum(onehot, axis=0) - 1), axis=1)
    target = flat_routes * capacity + ranks
    selector = (
        target[None, :] == jnp.arange(experts_all * capacity, dtype=jnp.int32)[:, None]
    ).astype(jnp.int32)
    selector = jnp.sum(selector.reshape(experts_all * capacity, batch_rows, topk), axis=2).astype(
        jnp.bfloat16
    )
    outgoing = jnp.dot(selector, normed, preferred_element_type=jnp.float32).astype(jnp.bfloat16)
    outgoing = outgoing.reshape(experts_all, capacity, width)
    received = lax.all_to_all(outgoing, ("grp", "dev"), split_axis=0, concat_axis=0, tiled=True)
    count = received.shape[0] * received.shape[1]
    gate_up = jnp.dot(
        received.reshape(count, width), expert_gate_up[0], preferred_element_type=jnp.float32
    )
    active = (jax.nn.silu(gate_up[:, :FF]) * gate_up[:, FF:]).astype(jnp.bfloat16)
    result = jnp.dot(active, expert_down[0], preferred_element_type=jnp.float32).astype(
        jnp.bfloat16
    )
    returned = lax.all_to_all(
        result.reshape(received.shape), ("grp", "dev"), split_axis=0, concat_axis=0, tiled=True
    )
    table = returned.reshape(experts_all * capacity, width)
    gathered = table[target].reshape(batch_rows, topk, width).astype(jnp.float32)
    combined = jnp.sum(gates[:, :, None] * gathered, axis=1)
    return (hidden + combined).astype(jnp.bfloat16)


def solution(mesh):
    placed = (
        P(("grp", "dev"), None),
        P(None, "dev", "grp"),
        P(None, "dev", "grp", None),
        P(None, "dev", "grp", None, None),
        P(None, "dev"),
        P("grp", None),
        P(),
        P(),
        P(("grp", "dev"), None),
        P(("grp", "dev"), None, None),
        P(("grp", "dev"), None, None),
    )
    return jax.shard_map(
        per_device, mesh=mesh, in_specs=placed, out_specs=P(("grp", "dev"), None), check_vma=False
    )
```

profile of v0, /device:TPU:0, one launch (start us, length us, event | category | flops | bytes accessed | tf_op | source)
XLA Modules:
  0.0 132.5 jit_solution(18427662515495649888)
XLA Ops:
  6.5 0.0 copy-start
  6.5 0.0 all-reduce.2.cloned.1.call-start
  6.5 0.9 iota_compare_fusion.2
  7.4 0.8 slice_convert_fusion
  8.3 0.9 copy.29
  9.2 0.2 fusion.34
  9.4 3.5 %fusion.43 = (f32[2,16,2,8]{3,2,1,0:T(2,128)S(1)}, f32[2,16,2,8,256]{4,3,2,1,0:T(8,128)S(1)}) fusion(bf16[2,16,2,8,128]{4,3,2,1,0:T(8,128)(2,1)S(1)} %bitcast.50, bf16[2,16,2,256,256]{4,3,2,1,0:T(8,128)(2,1)} %param.14, pred[2,16,256]{2,1,0:T(8,128)(4,1)S(1)} %iota_compare_fusion.2), kind=kOutput, calls=%fused_computation.58 | convolution fusion | flops 33947136 | bytes 4859904 | tf_op jit(solution)/shard_map/hrkgd,hrksd->hrkgs/dot_general | solution.py:34
  12.9 2.9 %fusion.25 = bf16[2,16,2,8,128]{4,3,2,1,0:T(8,128)(2,1)S(1)} fusion(bf16[2,16,2,256,256]{4,3,2,1,0:T(8,128)(2,1)} %param.14, f32[2,16,2,8,256]{4,3,2,1,0:T(8,128)S(1)} %get-tuple-element.12, f32[2,16,2,8]{3,2,1,0:T(2,128)S(1)} %get-tuple-element.6, f32[2,16,2,128]{3,2,1,0:T(2,128)S(1)} %get-tuple-element.7, f32[2,16,2,8]{3,2,1,0:T(2,128)S(1)} %get-tuple-element.5), kind=kOutput, calls=%fused_computation.18 | convolution fusion | flops 34013184 | bytes 4886528 | tf_op jit(solution)/shard_map/hrkgs,hrksd->hrkgd/dot_general | solution.py:60
  15.9 0.1 dot_general.29
  15.9 0.0 copy-start.3
  16.0 0.0 copy-start.4
  16.0 0.0 copy-start.2
  16.0 5.7 %fusion = f32[2,16,2048]{2,1,0:T(8,128)} fusion(bf16[2,16,2048]{2,1,0:T(8,128)(2,1)S(1)} %dot_general.29, bf16[2048,2048]{1,0:T(8,128)(2,1)} %param.16), kind=kOutput, calls=%fused_computation.2 | convolution fusion | flops 268435456 | bytes 8781824 | tf_op jit(solution)/shard_map/dot_general | solution.py:72
  21.6 0.0 all-reduce.2.cloned.1.call-update
  21.7 0.0 copy-done.3
  21.7 0.1 copy.25
  21.7 0.1 eq.29
  21.8 0.0 copy-done.4
  21.9 0.1 fusion.33
  21.9 0.2 reduce_window_sum.11
  22.1 0.2 select_reduce_fusion
  22.3 0.1 reduce_sum.62
  22.4 0.1 convert_reduce_fusion
  22.5 25.6 %all-reduce.2.cloned.1.call-done = f32[2,16,2048]{2,1,0:T(8,128)} async-done(((f32[2,16,2048]{2,1,0:T(8,128)}), f32[2,16,2048]{2,1,0:T(8,128)}) %all-reduce.2.cloned.1.call-update) | async-done | bytes 262160 | tf_op jit(solution)/shard_map/psum | solution.py:75
  48.1 0.0 copy-done.2
  48.1 1.0 multiply_reduce_fusion
  49.1 1.0 multiply_convert_fusion
  50.1 1.5 %convolution_convert_fusion = bf16[256,2048]{1,0:T(8,128)(2,1)} fusion(bf16[16,2048]{1,0:T(8,128)(2,1)S(1)} %multiply_convert_fusion, s32[256,16]{0,1:T(8,128)S(1)} %convert_reduce_fusion), kind=kOutput, calls=%fused_computation.13 | convolution fusion | flops 17305600 | bytes 1130496 | tf_op jit(solution)/shard_map/dot_general | solution.py:101
  51.6 2.5 %reshape.112 = bf16[128,2,2048]{2,1,0:T(2,128)(2,1)} reshape(bf16[256,2048]{1,0:T(8,128)(2,1)} %convolution_convert_fusion) | data formatting | bytes 2097152 | tf_op jit(solution)/shard_map/reshape | solution.py:102
  54.2 28.3 %all_to_all.10 = bf16[128,2,2048]{2,1,0:T(2,128)(2,1)} all-to-all(bf16[128,2,2048]{2,1,0:T(2,128)(2,1)} %reshape.112), channel_id=1, replica_groups=mesh['grp'=2,'dev'=64] {'grp','dev'}, dimensions={0} | all-to-all | bytes 2097152 | tf_op jit(solution)/shard_map/all_to_all | solution.py:103
  82.4 2.3 %reshape.113 = bf16[256,2048]{1,0:T(8,128)(2,1)} reshape(bf16[128,2,2048]{2,1,0:T(2,128)(2,1)} %all_to_all.10) | data formatting | bytes 2097152 | tf_op jit(solution)/shard_map/reshape | solution.py:106
  84.7 4.9 %fusion.2 = f32[256,1536]{1,0:T(8,128)S(1)} fusion(bf16[256,2048]{1,0:T(8,128)(2,1)} %reshape.113, bf16[1,2048,1536]{2,1,0:T(8,128)(2,1)} %param.20), kind=kOutput, calls=%fused_computation.4 | convolution fusion | flops 1610612736 | bytes 8912896 | tf_op jit(solution)/shard_map/dot_general | solution.py:105
  89.6 0.0 copy-done
  89.6 2.0 %fusion.10 = bf16[256,2048]{1,0:T(8,128)(2,1)} fusion(bf16[1,768,2048]{2,1,0:T(8,128)(2,1)S(1)} %copy-done, f32[256,1536]{1,0:T(8,128)S(1)} %fusion.2), kind=kOutput, calls=%fused_computation.12 | convolution fusion | flops 807010304 | bytes 5767168 | tf_op jit(solution)/shard_map/dot_general | solution.py:109
  91.7 2.5 %reshape.114 = bf16[128,2,2048]{2,1,0:T(2,128)(2,1)} reshape(bf16[256,2048]{1,0:T(8,128)(2,1)} %fusion.10) | data formatting | bytes 2097152 | tf_op jit(solution)/shard_map/reshape | solution.py:113
  94.2 5.8 %all-to-all-start.1 = ((bf16[128,2,2048]{2,1,0:T(2,128)(2,1)}), bf16[128,2,2048]{2,1,0:T(2,128)(2,1)}, u32[]{:S(2)}, u32[]{:S(2)}) async-start(bf16[128,2,2048]{2,1,0:T(2,128)(2,1)} %reshape.114), calls=%async_computation.1 | async-start | bytes 2097152 | tf_op jit(solution)/shard_map/all_to_all | solution.py:112
  100.0 0.1 copy.22
  100.1 0.1 reshape.125
  100.2 0.1 mul.100
  100.3 1.2 fusion.44
  101.5 1.3 gather_fusion.1
  102.8 0.0 copy-start.1
  102.8 0.1 reshape.128
  102.9 0.1 copy.23
  103.0 0.1 copy.24
  103.0 14.6 %all-to-all-done.1 = bf16[128,2,2048]{2,1,0:T(2,128)(2,1)} async-done(((bf16[128,2,2048]{2,1,0:T(2,128)(2,1)}), bf16[128,2,2048]{2,1,0:T(2,128)(2,1)}, u32[]{:S(2)}, u32[]{:S(2)}) %all-to-all-start.1) | async-done | bytes 1048608 | tf_op jit(solution)/shard_map/all_to_all | solution.py:112
  117.7 2.3 %reshape.115 = bf16[256,2048]{1,0:T(8,128)(2,1)} reshape(bf16[128,2,2048]{2,1,0:T(2,128)(2,1)} %all-to-all-done.1) | data formatting | bytes 2097152 | tf_op jit(solution)/shard_map/reshape | solution.py:115
  119.9 3.6 %gather_fusion = bf16[128,2048]{1,0:T(8,128)(2,1)} fusion(bf16[256,2048]{1,0:T(8,128)(2,1)} %reshape.115, s32[1024]{0:T(1024)S(1)} %pad_clamp_fusion), kind=kCustom, calls=%fused_computation | custom fusion | bytes 1049088 | tf_op jit(solution)/shard_map/gather | solution.py:116
  123.5 1.5 %fusion.28 = f32[16,2048]{1,0:T(8,128)S(1)} fusion(bf16[128,2048]{1,0:T(8,128)(2,1)} %gather_fusion, f32[16,8]{1,0:T(8,128)S(1)} %copy.24), kind=kLoop, calls=%fused_computation.20 | loop fusion | flops 753664 | bytes 655872 | tf_op jit(solution)/shard_map/reduce_sum | solution.py:117
  125.0 0.0 copy-done.1
  125.0 0.7 add_convert_fusion
  (9 shorter events, 0.1 us)
Async XLA Ops:
  6.5 83.1 %copy-start = (bf16[1,768,2048]{2,1,0:T(8,128)(2,1)S(1)}, bf16[1,768,2048]{2,1,0:T(8,128)(2,1)}, u32[]{:S(2)}) copy-start(bf16[1,768,2048]{2,1,0:T(8,128)(2,1)} %param.21) | copy-start | bytes 9437188
  6.5 41.5 %all-reduce.2.cloned.1.call-start = ((), (), s32[]{:S(2)}) async-start(), calls=%async_computation.2 | async-start | bytes 524288 | tf_op jit(solution)/shard_map/psum | solution.py:75
  15.9 5.7 %copy-start.3 = (s32[16,8]{0,1:T(8,128)S(1)}, s32[16,8]{0,1:T(8,128)}, u32[]{:S(2)}) copy-start(s32[16,8]{0,1:T(8,128)} %param.19) | copy-start | bytes 1540
  16.0 5.9 %copy-start.4 = (bf16[2048]{0:T(1024)(128)(2,1)S(1)}, bf16[2048]{0:T(1024)(128)(2,1)}, u32[]{:S(2)}) copy-start(bf16[2048]{0:T(1024)(128)(2,1)} %param.17) | copy-start | bytes 12292
  16.0 32.1 %copy-start.2 = (bf16[16,2048]{1,0:T(8,128)(2,1)S(1)}, bf16[16,2048]{1,0:T(8,128)(2,1)}, u32[]{:S(2)}) copy-start(bf16[16,2048]{1,0:T(8,128)(2,1)} %param.11) | copy-start | bytes 196612
  94.2 23.5 %all-to-all-start.1 = ((bf16[128,2,2048]{2,1,0:T(2,128)(2,1)}), bf16[128,2,2048]{2,1,0:T(2,128)(2,1)}, u32[]{:S(2)}, u32[]{:S(2)}) async-start(bf16[128,2,2048]{2,1,0:T(2,128)(2,1)} %reshape.114), calls=%async_computation.1 | async-start | bytes 2097152 | tf_op jit(solution)/shard_map/all_to_all | solution.py:112
  102.8 22.3 %copy-start.1 = (f32[2,16,2048]{2,1,0:T(8,128)S(1)}, f32[2,16,2048]{2,1,0:T(8,128)}, u32[]{:S(2)}) copy-start(f32[2,16,2048]{2,1,0:T(8,128)} %all-reduce.2.cloned.1.call-done) | copy-start | bytes 786436
Sparse Core Ops, SparseCore 0:
  21.8 26.2 all-reduce.1
where the time goes:
time: 133 us
  waiting for transfers between devices  40.2 us (30%)
  blocking collectives  28.3 us (21%)
  matrix products  21.9 us (16%)
  local copies, waits for them, and re-layouts  16.2 us (12%)
  between operations  13.6 us (10%)
  other arithmetic  6.56 us (5%)
  starting transfers between devices  5.78 us (4%)
    all_to_all x1, blocking collectives, per_device(): lax.all_to_all(outgoing, ('grp', 'dev'), split_axis=0, concat_axis=0, til...  28.3 us
    psum x1, waiting for transfers between devices, per_device(): summed = lax.psum(partial_value, 'grp')  25.6 us
    all_to_all x1, waiting for transfers between devices, per_device(): lax.all_to_all(result.reshape(received.shape), ('grp', 'dev'), split_axis...  14.6 us
    all_to_all x1, starting transfers between devices, per_device(): lax.all_to_all(result.reshape(received.shape), ('grp', 'dev'), split_axis...  5.78 us
    dot_general x1, matrix products, per_device(): jnp.dot(attended, out_weight, preferred_element_type=jnp.float32)  5.65 us
    dot_general x1, matrix products, per_device(): jnp.dot(received.reshape(count, width), expert_gate_up[0], preferred_elem...  4.9 us
    gather x1, local copies, waits for them, and re-layouts, per_device(): table[target].reshape(batch_rows, topk, width).astype(jnp.float32)  3.59 us
    dot_general x1, matrix products, per_device(): jnp.einsum('hrkgd,hrksd->hrkgs', query_vector, key_value_cache[..., :HEAD...  3.5 us
  transfers between devices with their start and end apart: 2, of which 2 were waited for; matrix products, arithmetic and copies ran while one was open for 3% of the time, Pallas kernels for 0%

commit v1 on v0

--- a/solution.py
+++ b/solution.py
@@ -1,3 +1,4 @@
+import functools
 import math
 import jax
 import jax.numpy as jnp
@@ -6,6 +7,14 @@
 
 HEAD_SIZE = 128
 FF = 768
+
+
+def shapes_pack(vector, axis_id):
+    t1 = jax.lax.all_gather(vector, axis_id)
+    return jnp.sum(t1, 0)
+
+
+take_roots = functools.partial(shapes_pack, axis_id="grp")
 
 
 def per_device(
@@ -72,7 +81,7 @@
     partial_value = jnp.dot(attended, out_weight, preferred_element_type=jnp.float32).reshape(
         halves, tokens, width
     )
-    summed = lax.psum(partial_value, "grp")
+    summed = take_roots(partial_value)
     projected = lax.dynamic_index_in_dim(summed, lax.axis_index("grp"), 0, keepdims=False)
     hidden = residual_in.astype(jnp.float32) + projected
     meansq = jnp.mean(hidden * hidden, axis=-1, keepdims=True)

time: 133 us -> 101 us (0.76)
  waiting for transfers between devices: 40.2 us -> 13.4 us
  between operations: 13.6 us -> 0.19 us
  blocking collectives: 28.3 us -> 31.7 us
  local copies, waits for them, and re-layouts: 16.2 us -> 18.8 us
  other arithmetic: 6.56 us -> 8.85 us
    psum x1 -> x0, waiting for transfers between devices: 25.6 us -> none  [per_device(): summed = lax.psum(partial_value, 'grp')]
    all_gather x0 -> x1, blocking collectives: none -> 2.31 us  [shapes_pack(): t1 = jax.lax.all_gather(vector, axis_id)]
    unnamed x12 -> x14, local copies, waits for them, and re-layouts: 1.03 us -> 2.4 us
  transfers between devices with their start and end apart: 2 -> 1, of which waited for: 2 -> 1; matrix products, arithmetic and copies ran while one was open for 3% -> 4% of each run, Pallas kernels for 0% -> 0%
where the time goes in v1:
time: 101 us
  blocking collectives  31.7 us (31%)
  matrix products  21.9 us (22%)
  local copies, waits for them, and re-layouts  18.8 us (19%)
  waiting for transfers between devices  13.4 us (13%)
  other arithmetic  8.85 us (9%)
  starting transfers between devices  5.78 us (6%)
    all_to_all x1, blocking collectives, per_device(): lax.all_to_all(outgoing, ('grp', 'dev'), split_axis=0, concat_axis=0, til...  29.4 us
    all_to_all x1, waiting for transfers between devices, per_device(): lax.all_to_all(result.reshape(received.shape), ('grp', 'dev'), split_axis...  13.4 us
    all_to_all x1, starting transfers between devices, per_device(): lax.all_to_all(result.reshape(received.shape), ('grp', 'dev'), split_axis...  5.78 us
    dot_general x1, matrix products, per_device(): jnp.dot(attended, out_weight, preferred_element_type=jnp.float32)  4.95 us
    dot_general x1, matrix products, per_device(): jnp.dot(received.reshape(count, width), expert_gate_up[0], preferred_elem...  4.9 us
    gather x1, local copies, waits for them, and re-layouts, per_device(): table[target].reshape(batch_rows, topk, width).astype(jnp.float32)  3.59 us
    dot_general x1, matrix products, per_device(): jnp.einsum('hrkgd,hrksd->hrkgs', query_vector, key_value_cache[..., :HEAD...  3.5 us
    dot_general x1, matrix products, per_device(): jnp.einsum('hrkgs,hrksd->hrkgd', weights, key_value_cache[..., HEAD_SIZE:...  2.91 us
  transfers between devices with their start and end apart: 1, of which 1 were waited for; matrix products, arithmetic and copies ran while one was open for 4% of the time, Pallas kernels for 0%

profile of v1, /device:TPU:0, one launch (start us, length us, event | category | flops | bytes accessed | tf_op | source)
XLA Modules:
  0.0 100.6 jit_solution(16549710308279374977)
XLA Ops:
  0.0 0.0 copy-start
  0.0 0.9 copy.30
  0.9 0.1 eq.29
  1.0 0.8 iota_compare_fusion.2
  1.8 1.3 %convert_element_type.58 = f32[2048]{0:T(1024)} convert(bf16[2048]{0:T(1024)(128)(2,1)} %param.17) | non-fusion elementwise | flops 2048 | bytes 12288 | tf_op jit(solution)/shard_map/convert_element_type | solution.py:88
  3.0 0.8 slice_convert_fusion
  3.8 0.1 fusion.33
  3.9 0.2 reduce_window_sum.11
  4.1 0.2 select_reduce_fusion
  4.2 0.0 copy-start.3
  4.2 0.5 copy-done.3
  4.8 0.1 reduce_sum.72
  4.9 0.6 broadcast_multiply_fusion
  5.5 0.7 convert_reduce_fusion
  6.2 0.9 copy.34
  7.1 0.2 fusion.34
  7.3 3.5 %fusion.43 = (f32[2,16,2,8]{3,2,1,0:T(2,128)S(1)}, f32[2,16,2,8,256]{4,3,2,1,0:T(8,128)S(1)}) fusion(bf16[2,16,2,8,128]{4,3,2,1,0:T(8,128)(2,1)S(1)} %bitcast.52, bf16[2,16,2,256,256]{4,3,2,1,0:T(8,128)(2,1)} %param.14, pred[2,16,256]{2,1,0:T(8,128)(4,1)S(1)} %iota_compare_fusion.2), kind=kOutput, calls=%fused_computation.58 | convolution fusion | flops 33947136 | bytes 4859904 | tf_op jit(solution)/shard_map/hrkgd,hrksd->hrkgs/dot_general | solution.py:43
  10.8 0.1 fusion.37
  10.9 2.9 %fusion.25 = bf16[2,16,2,8,128]{4,3,2,1,0:T(8,128)(2,1)S(1)} fusion(bf16[2,16,2,256,256]{4,3,2,1,0:T(8,128)(2,1)} %param.14, f32[2,16,2,8,256]{4,3,2,1,0:T(8,128)S(1)} %get-tuple-element.12, f32[2,16,2,8]{3,2,1,0:T(2,128)S(1)} %get-tuple-element.6, f32[2,16,2,128]{3,2,1,0:T(2,128)S(1)} %get-tuple-element.7, f32[2,16,2,8]{3,2,1,0:T(2,128)S(1)} %get-tuple-element.5), kind=kOutput, calls=%fused_computation.18 | convolution fusion | flops 34013184 | bytes 4886528 | tf_op jit(solution)/shard_map/hrkgs,hrksd->hrkgd/dot_general | solution.py:69
  13.8 0.1 reshape.115
  13.9 0.0 copy-start.1
  13.9 5.0 %fusion = f32[2,16,2048]{2,1,0:T(8,128)S(1)} fusion(bf16[2,16,2048]{2,1,0:T(8,128)(2,1)S(1)} %reshape.115, bf16[2048,2048]{1,0:T(8,128)(2,1)} %param.16), kind=kOutput, calls=%fused_computation.2 | convolution fusion | flops 268435456 | bytes 8781824 | tf_op jit(solution)/shard_map/dot_general | solution.py:81
  18.8 2.3 %all-gather = f32[4,16,2048]{2,1,0:T(8,128)} all-gather(f32[2,16,2048]{2,1,0:T(8,128)S(1)} %fusion), channel_id=2, replica_groups=mesh['grp'=2,'dev'=64] {'grp'}, dimensions={0}, use_global_device_ids=true | all-gather | bytes 786432 | tf_op jit(solution)/shard_map/all_gather | solution.py:13
  21.1 1.1 %reduce_sum.68 = f32[2,16,2048]{2,1,0:T(8,128)S(1)} reduce(f32[2,2,16,2048]{3,2,1,0:T(8,128)} %bitcast.50, f32[]{:T(128)} %constant.19.clone.1), dimensions={0}, to_apply=%region_1.2 | reduce | flops 65536 | bytes 786436 | tf_op jit(solution)/shard_map/reduce_sum | solution.py:14
  22.3 0.0 copy-done.1
  22.3 0.1 multiply_reduce_fusion
  22.4 0.8 multiply_convert_fusion
  23.2 2.2 %convolution_convert_fusion = bf16[256,2048]{1,0:T(8,128)(2,1)} fusion(bf16[16,2048]{1,0:T(8,128)(2,1)S(1)} %multiply_convert_fusion, s32[256,16]{0,1:T(8,128)} %convert_reduce_fusion), kind=kOutput, calls=%fused_computation.13 | convolution fusion | flops 17305600 | bytes 1130496 | tf_op jit(solution)/shard_map/dot_general | solution.py:110
  25.4 2.5 %reshape.117 = bf16[128,2,2048]{2,1,0:T(2,128)(2,1)} reshape(bf16[256,2048]{1,0:T(8,128)(2,1)} %convolution_convert_fusion) | data formatting | bytes 2097152 | tf_op jit(solution)/shard_map/reshape | solution.py:111
  28.0 29.4 %all_to_all.10 = bf16[128,2,2048]{2,1,0:T(2,128)(2,1)} all-to-all(bf16[128,2,2048]{2,1,0:T(2,128)(2,1)} %reshape.117), channel_id=1, replica_groups=mesh['grp'=2,'dev'=64] {'grp','dev'}, dimensions={0} | all-to-all | bytes 2097152 | tf_op jit(solution)/shard_map/all_to_all | solution.py:112
  57.3 2.3 %reshape.118 = bf16[256,2048]{1,0:T(8,128)(2,1)} reshape(bf16[128,2,2048]{2,1,0:T(2,128)(2,1)} %all_to_all.10) | data formatting | bytes 2097152 | tf_op jit(solution)/shard_map/reshape | solution.py:115
  59.6 4.9 %fusion.2 = f32[256,1536]{1,0:T(8,128)S(1)} fusion(bf16[256,2048]{1,0:T(8,128)(2,1)} %reshape.118, bf16[1,2048,1536]{2,1,0:T(8,128)(2,1)} %param.20), kind=kOutput, calls=%fused_computation.4 | convolution fusion | flops 1610612736 | bytes 8912896 | tf_op jit(solution)/shard_map/dot_general | solution.py:114
  64.5 0.0 copy-done
  64.5 0.0 copy-start.2
  64.5 2.0 %fusion.10 = bf16[256,2048]{1,0:T(8,128)(2,1)} fusion(bf16[1,768,2048]{2,1,0:T(8,128)(2,1)S(1)} %copy-done, f32[256,1536]{1,0:T(8,128)S(1)} %fusion.2), kind=kOutput, calls=%fused_computation.12 | convolution fusion | flops 807010304 | bytes 5767168 | tf_op jit(solution)/shard_map/dot_general | solution.py:118
  66.6 2.5 %reshape.119 = bf16[128,2,2048]{2,1,0:T(2,128)(2,1)} reshape(bf16[256,2048]{1,0:T(8,128)(2,1)} %fusion.10) | data formatting | bytes 2097152 | tf_op jit(solution)/shard_map/reshape | solution.py:122
  69.1 5.8 %all-to-all-start.1 = ((bf16[128,2,2048]{2,1,0:T(2,128)(2,1)}), bf16[128,2,2048]{2,1,0:T(2,128)(2,1)}, u32[]{:S(2)}, u32[]{:S(2)}) async-start(bf16[128,2,2048]{2,1,0:T(2,128)(2,1)} %reshape.119), calls=%async_computation.1 | async-start | bytes 2097152 | tf_op jit(solution)/shard_map/all_to_all | solution.py:121
  74.9 0.0 copy-done.2
  74.9 0.1 copy.27
  75.0 0.1 reshape.130
  75.1 1.3 %mul.100 = s32[128,1]{0,1:T(1,128)} reshape(s32[16,8]{1,0:T(8,128)} %get-tuple-element.9) | data formatting | bytes 1024 | tf_op jit(solution)/shard_map/mul | solution.py:103
  76.4 1.2 %fusion.44 = f32[16,128]{1,0:T(8,128)S(1)} fusion(bf16[16,2048]{1,0:T(8,128)(2,1)S(1)} %multiply_convert_fusion, bf16[2048,128]{1,0:T(8,128)(2,1)} %param.18), kind=kOutput, calls=%fused_computation.59 | convolution fusion | flops 8388608 | bytes 598016 | tf_op jit(solution)/shard_map/dot_general | solution.py:91
  77.6 0.0 copy-start.4
  77.6 0.0 copy-start.5
  77.6 1.2 %gather_fusion.1 = f32[128]{0:T(128)S(1)} fusion(f32[16,128]{1,0:T(8,128)S(1)} %fusion.44, s32[128]{0:T(128)S(1)} %reshape.130), kind=kCustom, calls=%fused_computation.1 | custom fusion | bytes 2048 | tf_op jit(solution)/shard_map/jit(take_along_axis)/gather | solution.py:92
  78.9 0.1 reshape.133
  78.9 0.1 copy.28
  79.1 0.1 copy.29
  79.1 0.0 copy-done.4
  79.1 0.0 copy-done.5
  79.2 13.4 %all-to-all-done.1 = bf16[128,2,2048]{2,1,0:T(2,128)(2,1)} async-done(((bf16[128,2,2048]{2,1,0:T(2,128)(2,1)}), bf16[128,2,2048]{2,1,0:T(2,128)(2,1)}, u32[]{:S(2)}, u32[]{:S(2)}) %all-to-all-start.1) | async-done | bytes 1048608 | tf_op jit(solution)/shard_map/all_to_all | solution.py:121
  92.6 2.3 %reshape.120 = bf16[256,2048]{1,0:T(8,128)(2,1)} reshape(bf16[128,2,2048]{2,1,0:T(2,128)(2,1)} %all-to-all-done.1) | data formatting | bytes 2097152 | tf_op jit(solution)/shard_map/reshape | solution.py:124
  94.8 3.6 %gather_fusion = bf16[128,2048]{1,0:T(8,128)(2,1)} fusion(bf16[256,2048]{1,0:T(8,128)(2,1)} %reshape.120, s32[1024]{0:T(1024)S(1)} %pad_clamp_fusion), kind=kCustom, calls=%fused_computation | custom fusion | bytes 1049088 | tf_op jit(solution)/shard_map/gather | solution.py:125
  98.4 1.5 %fusion.28 = f32[16,2048]{1,0:T(8,128)S(1)} fusion(bf16[128,2048]{1,0:T(8,128)(2,1)} %gather_fusion, f32[16,8]{1,0:T(8,128)S(1)} %copy.29), kind=kLoop, calls=%fused_computation.20 | loop fusion | flops 753664 | bytes 655872 | tf_op jit(solution)/shard_map/reduce_sum | solution.py:126
  99.9 0.7 add_convert_fusion
  (6 shorter events, 0.1 us)
Async XLA Ops:
  0.0 64.5 %copy-start = (bf16[1,768,2048]{2,1,0:T(8,128)(2,1)S(1)}, bf16[1,768,2048]{2,1,0:T(8,128)(2,1)}, u32[]{:S(2)}) copy-start(bf16[1,768,2048]{2,1,0:T(8,128)(2,1)} %param.21) | copy-start | bytes 9437188
  4.2 0.6 copy-start.3
  13.9 8.4 %copy-start.1 = (bf16[16,2048]{1,0:T(8,128)(2,1)S(1)}, bf16[16,2048]{1,0:T(8,128)(2,1)}, u32[]{:S(2)}) copy-start(bf16[16,2048]{1,0:T(8,128)(2,1)} %param.11) | copy-start | bytes 196612
  64.5 10.4 %copy-start.2 = (s32[16,8]{0,1:T(8,128)S(1)}, s32[16,8]{0,1:T(8,128)}, u32[]{:S(2)}) copy-start(s32[16,8]{0,1:T(8,128)} %param.19) | copy-start | bytes 1540
  69.1 23.5 %all-to-all-start.1 = ((bf16[128,2,2048]{2,1,0:T(2,128)(2,1)}), bf16[128,2,2048]{2,1,0:T(2,128)(2,1)}, u32[]{:S(2)}, u32[]{:S(2)}) async-start(bf16[128,2,2048]{2,1,0:T(2,128)(2,1)} %reshape.119), calls=%async_computation.1 | async-start | bytes 2097152 | tf_op jit(solution)/shard_map/all_to_all | solution.py:121
  77.6 1.5 %copy-start.4 = (s32[128]{0:T(128)S(1)}, s32[128]{0:T(128)}, u32[]{:S(2)}) copy-start(s32[128]{0:T(128)} %copy-done.3) | copy-start | bytes 1540
  77.6 1.5 %copy-start.5 = (s32[128,1]{0,1:T(1,128)S(1)}, s32[128,1]{0,1:T(1,128)}, u32[]{:S(2)}) copy-start(s32[128,1]{0,1:T(1,128)} %mul.100) | copy-start | bytes 1540
